TPU v7x, 32 devices: a whole 2x2x4 slice. The times are simulated.
32 devices in a mesh: hap: 2 (over x), snp: 16 (over z, y, core).
Axes of the slice: x: 2, y: 2, z: 4, core: 2. Of those that a mesh axis runs over, the one named last changes fastest.
Arguments:
- packed_panel: int32 [96, 16384], P('hap', 'snp'), may hold values from 0 to 8191, as said below
- components: bfloat16 [64, 1248], P(None, 'hap'), may hold values from -0.15625 to 0.15625
- bounds: int32 [2, 16384], P(None, 'snp'), may hold values from 0 to 16383, as said below
- band_width: int32 [16384], P('snp'), may hold values from 1 to 256
Outputs:
- ld_scores: float32 [16384], P('snp')
Inputs may be any that keep to these rules, and one draw needn't show every extreme that they name: Bit j of packed_panel[w, s] (j from 0 to 12) is the allele of haplotype 13 w + j at SNP s; higher bits are zero. LD blocks are consecutive runs of 1 to 2048 SNPs that cover all SNPs in order; bounds[0, s] and bounds[1, s] are the first and last SNP of the block holding s.
All inputs are finite; a program needn't handle non-finite values.
Results may differ from a plain program's by a relative error of at most 0.00074.
Values may be sent and summed in bfloat16 or wider, within the bound.
No kernel may reach another device: no remote copies, remote signals or barrier semaphores. Data moves between devices by JAX's collectives and lax.ppermute only.
A program may use at most 64 MiB of HBM per device.

v0:
```python
import jax
import jax.numpy as jnp
from jax import lax
from jax.sharding import PartitionSpec as P

epsilon = 1e-06


def padded_2(block, sides, width):
    for axis, dim in sides:
        count = lax.axis_size(axis)
        forward = [(i, i + 1) for i in range(count - 1)]
        backward = [(target, source) for source, target in forward]
        low = lax.ppermute(
            lax.slice_in_dim(block, block.shape[dim] - width, None, axis=dim), axis, forward
        )
        high = lax.ppermute(lax.slice_in_dim(block, 0, width, axis=dim), axis, backward)
        block = jnp.concatenate([low, block, high], axis=dim)
    return block


def unpack(packed):
    shifts = jnp.arange(13, dtype=jnp.int32)
    bit_values = jnp.bitwise_and(jnp.right_shift(packed[:, None, :], shifts[None, :, None]), 1)
    return bit_values.reshape(packed.shape[0] * 13, packed.shape[1]).astype(jnp.bfloat16)


def project(components, packed_panel):
    column_count = packed_panel.shape[1]
    block_size = min(256, column_count)
    zeroed = jnp.zeros((components.shape[0], column_count), jnp.float32)

    def add_block(block_index, accumulated):
        packed = lax.dynamic_slice_in_dim(packed_panel, block_index * block_size, block_size, 1)
        product = jnp.dot(components, unpack(packed), preferred_element_type=jnp.float32)
        return lax.dynamic_update_slice_in_dim(accumulated, product, block_index * block_size, 1)

    return lax.fori_loop(0, column_count // block_size, add_block, zeroed)


def standardize(factor):
    average = jnp.mean(factor, axis=1, keepdims=True)
    centered = factor - average
    variance = jnp.mean(centered * centered, axis=1, keepdims=True)
    return (centered * lax.rsqrt(variance + epsilon)).astype(jnp.bfloat16)


def band_scores(padded, inverse, bounds, band_width, offset, start_row, row_count, reach_width):
    component_count = padded.shape[0]
    block_size = min(256, row_count)

    def block_scores(block_index):
        first_row = start_row + block_index * block_size
        row_part = lax.dynamic_slice_in_dim(padded, first_row + reach_width, block_size, 1)
        column_part = lax.dynamic_slice_in_dim(padded, first_row, block_size + 2 * reach_width, 1)
        inverse_rows = lax.dynamic_slice_in_dim(inverse, first_row + reach_width, block_size, 0)
        inverse_columns = lax.dynamic_slice_in_dim(
            inverse, first_row, block_size + 2 * reach_width, 0
        )
        block_first = lax.dynamic_slice_in_dim(bounds[0], first_row, block_size, 0)
        block_last = lax.dynamic_slice_in_dim(bounds[1], first_row, block_size, 0)
        row_reach = lax.dynamic_slice_in_dim(band_width, first_row, block_size, 0)
        inner_products = lax.dot_general(
            row_part, column_part, (((0,), (0,)), ((), ())), preferred_element_type=jnp.float32
        )
        correlation = (
            inner_products
            * (1.0 / component_count)
            * inverse_rows[:, None]
            * inverse_columns[None, :]
        )
        row_position = offset + first_row + jnp.arange(block_size, dtype=jnp.int32)
        column_position = (
            offset
            + first_row
            - reach_width
            + jnp.arange(block_size + 2 * reach_width, dtype=jnp.int32)
        )
        window_low = jnp.maximum(block_first, row_position - row_reach)
        window_high = jnp.minimum(block_last, row_position + row_reach)
        inside = (
            (column_position[None, :] >= window_low[:, None])
            & (column_position[None, :] <= window_high[:, None])
            & (column_position[None, :] != row_position[:, None])
        )
        squared_sum = jnp.sum(jnp.where(inside, correlation * correlation, 0.0), axis=1)
        window_count = jnp.sum(inside.astype(jnp.float32), axis=1)
        return component_count * squared_sum / jnp.maximum(window_count, 1.0)

    blocks = jnp.arange(row_count // block_size, dtype=jnp.int32)
    return lax.map(block_scores, blocks).reshape(row_count)


def on_device(packed_panel, components, bounds, band_width):
    partial_factor = project(components, packed_panel)
    column_count = partial_factor.shape[1]
    factor = lax.psum(partial_factor, "hap")
    component_rows = lax.all_to_all(factor, "snp", split_axis=0, concat_axis=1, tiled=True)
    scaled = standardize(component_rows)
    normed = lax.all_to_all(scaled, "snp", split_axis=1, concat_axis=0, tiled=True)
    reach_width = column_count // 4
    padded = padded_2(normed, (("snp", 1),), reach_width)
    inverse = lax.rsqrt(jnp.mean(jnp.square(padded.astype(jnp.float32)), axis=0) + epsilon)
    offset = lax.axis_index("snp") * column_count
    share_rows = column_count // lax.axis_size("hap")
    own_scores = band_scores(
        padded,
        inverse,
        bounds,
        band_width,
        offset,
        lax.axis_index("hap") * share_rows,
        share_rows,
        reach_width,
    )
    return lax.all_gather(own_scores, "hap", axis=0, tiled=True)


def solution(mesh):
    in_specs = (P("hap", "snp"), P(None, "hap"), P(None, "snp"), P("snp"))
    out_specs = P("snp")
    return jax.shard_map(
        on_device, mesh=mesh, in_specs=in_specs, out_specs=out_specs, check_vma=False
    )
```

profile of v0, /device:TPU:13, one launch (start us, length us, event | category | flops | bytes accessed | tf_op | source)
XLA Modules:
  0.0 91.0 jit_solution(2346714453307130350)
XLA Ops:
  6.6 0.9 copy-done
  7.4 5.6 %while.25 = (s32[]{:T(128)}, f32[64,1024]{1,0:T(8,128)S(1)}, s32[48,1024]{1,0:T(8,128)}, bf16[64,624]{1,0:T(8,128)(2,1)S(1)}, s32[]{:T(128)}, /*index=5*/s32[]{:T(128)}, s32[]{:T(128)}, s32[]{:T(128)}) while((s32[]{:T(128)}, f32[64,1024]{1,0:T(8,128)S(1)}, s32[48,1024]{1,0:T(8,128)}, bf16[64,624]{1,0:T(8,128)(2,1)S(1)}, s32[]{:T(128)}, ...), condition=%wide.region_1.0_spmd, body=%wide.region_0.0_spmd.sunk | while | flops 20926468 | bytes 2862539 | solution.py:38
  7.4 0.8 constant_dynamic-slice_fusion.6
  8.5 0.3 fusion.22
  8.8 0.8 constant_dynamic-slice_fusion.6
  9.9 0.3 fusion.22
  10.3 0.8 constant_dynamic-slice_fusion.6
  11.4 0.3 fusion.22
  11.7 0.8 constant_dynamic-slice_fusion.6
  12.8 0.3 fusion.22
  13.1 0.8 all_to_all.22
  13.9 24.1 %all-reduce.2.cloned.1.call-done = f32[16,4,1024]{2,1,0:T(4,128)} async-done(((f32[16,4,1024]{2,1,0:T(4,128)}), f32[16,4,1024]{2,1,0:T(4,128)}) %all-reduce.2.cloned.1.call-update) | async-done | bytes 262160 | tf_op jit(solution)/shard_map/psum | solution.py:97
  37.9 14.8 %all_to_all.29 = f32[16,4,1024]{2,1,0:T(4,128)S(1)} all-to-all(f32[16,4,1024]{2,1,0:T(4,128)} %all-reduce.2.cloned.1.call-done), channel_id=1, replica_groups=mesh['hap'=2,'snp'=16] {'snp'}, dimensions={0} | all-to-all | bytes 524288 | tf_op jit(solution)/shard_map/all_to_all | solution.py:98
  52.7 0.3 reduce_sum.51
  53.0 0.3 multiply_reduce_fusion.1
  53.3 0.1 fusion.11
  53.5 9.9 %all_to_all.30 = bf16[4,16,1024]{2,0,1:T(4,128)(2,1)S(1)} all-to-all(bf16[4,16,1024]{2,0,1:T(4,128)(2,1)S(1)} %fusion.11), channel_id=1, replica_groups=mesh['hap'=2,'snp'=16] {'snp'}, dimensions={1} | all-to-all | bytes 262144 | tf_op jit(solution)/shard_map/all_to_all | solution.py:100
  63.4 3.7 %collective-permute-start = (bf16[64,256]{1,0:T(8,128)(2,1)S(1)}, bf16[64,256]{1,0:T(8,128)(2,1)S(1)}, u32[]{:S(2)}, u32[]{:S(2)}) collective-permute-start(bf16[64,256]{1,0:T(8,128)(2,1)S(1)} %get-tuple-element.232), channel_id=1, source_target_pairs={{0,1},{1,2},{2,3},{3,4},{4,5},{5,6},{6,7},{7,8},{8,9},{9,10},{10,1... | collective-permute-start | bytes 98312 | tf_op jit(solution)/shard_map/ppermute | solution.py:14
  67.1 1.9 %collective-permute-start.1 = (bf16[64,256]{1,0:T(8,128)(2,1)S(1)}, bf16[64,256]{1,0:T(8,128)(2,1)S(1)}, u32[]{:S(2)}, u32[]{:S(2)}) collective-permute-start(bf16[64,256]{1,0:T(8,128)(2,1)S(1)} %get-tuple-element.231), channel_id=1, source_target_pairs={{1,0},{2,1},{3,2},{4,3},{5,4},{6,5},{7,6},{8,7},{9,8},{10,9},{11,1... | collective-permute-start | bytes 98312 | tf_op jit(solution)/shard_map/ppermute | solution.py:17
  69.1 4.2 %collective-permute-done.1 = bf16[64,256]{1,0:T(8,128)(2,1)S(1)} collective-permute-done((bf16[64,256]{1,0:T(8,128)(2,1)S(1)}, bf16[64,256]{1,0:T(8,128)(2,1)S(1)}, u32[]{:S(2)}, u32[]{:S(2)}) %collective-permute-start.1) | collective-permute-done | bytes 32800 | tf_op jit(solution)/shard_map/ppermute | solution.py:17
  73.4 0.7 copy-done.1
  74.0 6.3 %while.26 = (s32[]{:T(128)}, f32[2,256]{1,0:T(2,128)S(1)}, s32[2]{0:T(128)S(1)}, s32[]{:T(128)}, s32[]{:T(128)}, /*index=5*/s32[2,1024]{1,0:T(2,128)S(1)}, s32[1...) while((s32[]{:T(128)}, f32[2,256]{1,0:T(2,128)S(1)}, ...), condition=%wide.region_9.10_spmd, body=%wide.region_6.9_spmd.sunk | while | flops 28510736 | bytes 194922 | solution.py:91
  74.0 0.6 dynamic_slice.80
  75.4 0.8 subtract_maximum_fusion.2
  76.3 0.5 fusion.26
  76.8 0.3 convert_reduce_fusion.2
  77.2 0.6 dynamic_slice.80
  78.5 0.8 subtract_maximum_fusion.2
  79.5 0.5 fusion.26
  80.0 0.3 convert_reduce_fusion.2
  80.4 3.2 %all-gather = f32[2,1,512]{2,1,0:T(1,128)S(1)} all-gather(f32[1,1,512]{2,1,0:T(1,128)S(1)} %reshape.97), channel_id=1, replica_groups=mesh['hap'=2,'snp'=16] {'hap'}, dimensions={0}, use_global_device_ids=true | all-gather | bytes 6144 | tf_op jit(solution)/shard_map/all_gather | solution.py:116
  83.6 0.6 copy.23
  (50 shorter events, 1.7 us)
Async XLA Ops:
  6.5 31.4 %all-reduce.2.cloned.1.call-start = ((), (), s32[]{:S(2)}) async-start(), calls=%async_computation.2 | async-start | bytes 524288 | tf_op jit(solution)/shard_map/psum | solution.py:97
  6.5 0.9 copy-start
  63.4 5.7 %collective-permute-start = (bf16[64,256]{1,0:T(8,128)(2,1)S(1)}, bf16[64,256]{1,0:T(8,128)(2,1)S(1)}, u32[]{:S(2)}, u32[]{:S(2)}) collective-permute-start(bf16[64,256]{1,0:T(8,128)(2,1)S(1)} %get-tuple-element.232), channel_id=1, source_target_pairs={{0,1},{1,2},{2,3},{3,4},{4,5},{5,6},{6,7},{7,8},{8,9},{9,10},{10,1... | collective-permute-start | bytes 98312 | tf_op jit(solution)/shard_map/ppermute | solution.py:14
  67.1 6.1 %collective-permute-start.1 = (bf16[64,256]{1,0:T(8,128)(2,1)S(1)}, bf16[64,256]{1,0:T(8,128)(2,1)S(1)}, u32[]{:S(2)}, u32[]{:S(2)}) collective-permute-start(bf16[64,256]{1,0:T(8,128)(2,1)S(1)} %get-tuple-element.231), channel_id=1, source_target_pairs={{1,0},{2,1},{3,2},{4,3},{5,4},{6,5},{7,6},{8,7},{9,8},{10,9},{11,1... | collective-permute-start | bytes 98312 | tf_op jit(solution)/shard_map/ppermute | solution.py:17
  73.3 0.7 copy-start.1
Sparse Core Ops, SparseCore 0:
  14.0 23.8 all-reduce.1
where the time goes:
time: 91.7 us; the launch traced here: 91 us
  waiting for transfers between devices  28.2 us (31%)
  blocking collectives  27.9 us (30%)
  between operations  13.5 us (15%)
  local copies, waits for them, and re-layouts  8.78 us (10%)
  starting transfers between devices  5.62 us (6%)
  other arithmetic  3.17 us (3%)
  matrix products  2.22 us (2%)
  loops' own time  1.59 us (2%)
    psum x1, waiting for transfers between devices, on_device(): factor = lax.psum(partial_factor, 'hap')  24.1 us
    all_to_all x1, blocking collectives, on_device(): lax.all_to_all(factor, 'snp', split_axis=0, concat_axis=1, tiled=True)  14.8 us
    all_to_all x1, blocking collectives, on_device(): lax.all_to_all(scaled, 'snp', split_axis=1, concat_axis=0, tiled=True)  9.91 us
    ppermute x1, waiting for transfers between devices, padded_2(): lax.ppermute(lax.slice_in_dim(block, 0, width, axis=dim), axis, backward)  4.16 us
    ppermute x1, starting transfers between devices, padded_2(): lax.ppermute(lax.slice_in_dim(block, block.shape[dim] - width, None, axis...  3.7 us
    dynamic_slice x4, local copies, waits for them, and re-layouts, add_block(): lax.dynamic_slice_in_dim(packed_panel, block_index * block_size, block_si...  3.23 us
    all_gather x1, blocking collectives, on_device(): return lax.all_gather(own_scores, 'hap', axis=0, tiled=True)  3.21 us
    unnamed x8, local copies, waits for them, and re-layouts  2.16 us
  transfers between devices with their start and end apart: 3, of which 2 were waited for; matrix products, arithmetic and copies ran while one was open for 0% of the time, Pallas kernels for 0%

commit v1 on v0

--- a/solution.py
+++ b/solution.py
@@ -4,6 +4,29 @@
 from jax.sharding import PartitionSpec as P
 
 epsilon = 1e-06
+
+
+def in_blocks(x, dim, peers):
+    lengths = x.shape
+    blocks = x.reshape(*lengths[:dim], peers, lengths[dim] // peers, *lengths[dim + 1 :])
+    return jnp.moveaxis(blocks, dim, 0)
+
+
+def laid_out(blocks, dim):
+    blocks = jnp.moveaxis(blocks, 0, dim)
+    shape = blocks.shape
+    return blocks.reshape(*shape[:dim], shape[dim] * shape[dim + 1], *shape[dim + 2 :])
+
+
+def pairwise_exchange(value, axis, split_dim, concat_dim):
+    size, here = (lax.axis_size(axis), lax.axis_index(axis))
+    blocks = in_blocks(value, split_dim, size)
+    outs = [blocks[here]]
+    for hop in range(1, size):
+        sent = blocks[here ^ hop]
+        outs.append(lax.ppermute(sent, axis, [(i, i ^ hop) for i in range(size)]))
+    blocks = jnp.stack(outs)[here ^ jnp.arange(size)]
+    return laid_out(blocks, concat_dim)
 
 
 def padded_2(block, sides, width):
@@ -95,7 +118,7 @@
     partial_factor = project(components, packed_panel)
     column_count = partial_factor.shape[1]
     factor = lax.psum(partial_factor, "hap")
-    component_rows = lax.all_to_all(factor, "snp", split_axis=0, concat_axis=1, tiled=True)
+    component_rows = pairwise_exchange(factor, "snp", 0, 1)
     scaled = standardize(component_rows)
     normed = lax.all_to_all(scaled, "snp", split_axis=1, concat_axis=0, tiled=True)
     reach_width = column_count // 4

time: 91.7 us -> 104 us (1.13)
  starting transfers between devices: 5.62 us -> 23.5 us
  blocking collectives: 27.9 us -> 17.5 us
  waiting for transfers between devices: 28.2 us -> 31 us
  local copies, waits for them, and re-layouts: 8.78 us -> 10.6 us
    ppermute x0 -> x15, starting transfers between devices: none -> 18 us  [pairwise_exchange(): outs.append(lax.ppermute(sent, axis, [(i, i ^ hop) for i in range(size)]))]
    all_to_all x1 -> x0, blocking collectives: 14.8 us -> none  [on_device(): lax.all_to_all(factor, 'snp', split_axis=0, concat_axis=1, tiled=True)]
    all_to_all x1, blocking collectives: 9.91 us -> 14.3 us  [on_device(): lax.all_to_all(scaled, 'snp', split_axis=1, concat_axis=0, tiled=True)]
    ppermute x0 -> x15, waiting for transfers between devices: none -> 2.81 us  [pairwise_exchange(): outs.append(lax.ppermute(sent, axis, [(i, i ^ hop) for i in range(size)]))]
    unnamed x8 -> x22, local copies, waits for them, and re-layouts: 2.16 us -> 2.27 us
  transfers between devices with their start and end apart: 3 -> 18, of which waited for: 2 -> 5; matrix products, arithmetic and copies ran while one was open for 0% -> 0% of each run, Pallas kernels for 0% -> 0%
where the time goes in v1:
time: 104 us; the launch traced here: 103 us
  waiting for transfers between devices  31 us (30%)
  starting transfers between devices  23.5 us (23%)
  blocking collectives  17.5 us (17%)
  between operations  13.6 us (13%)
  local copies, waits for them, and re-layouts  10.6 us (10%)
  other arithmetic  3.17 us (3%)
  matrix products  2.22 us (2%)
  loops' own time  1.6 us (2%)
    psum x1, waiting for transfers between devices, on_device(): factor = lax.psum(partial_factor, 'hap')  24 us
    ppermute x15, starting transfers between devices, pairwise_exchange(): outs.append(lax.ppermute(sent, axis, [(i, i ^ hop) for i in range(size)]))  18 us
    all_to_all x1, blocking collectives, on_device(): lax.all_to_all(scaled, 'snp', split_axis=1, concat_axis=0, tiled=True)  14.3 us
    ppermute x1, waiting for transfers between devices, padded_2(): lax.ppermute(lax.slice_in_dim(block, 0, width, axis=dim), axis, backward)  4.16 us
    ppermute x1, starting transfers between devices, padded_2(): lax.ppermute(lax.slice_in_dim(block, block.shape[dim] - width, None, axis...  3.61 us
    dynamic_slice x4, local copies, waits for them, and re-layouts, add_block(): lax.dynamic_slice_in_dim(packed_panel, block_index * block_size, block_si...  3.23 us
    all_gather x1, blocking collectives, on_device(): return lax.all_gather(own_scores, 'hap', axis=0, tiled=True)  3.21 us
    ppermute x15, waiting for transfers between devices, pairwise_exchange(): outs.append(lax.ppermute(sent, axis, [(i, i ^ hop) for i in range(size)]))  2.81 us
  transfers between devices with their start and end apart: 18, of which 5 were waited for; matrix products, arithmetic and copies ran while one was open for 0% of the time, Pallas kernels for 0%

profile of v1, /device:TPU:13, one launch (start us, length us, event | category | flops | bytes accessed | tf_op | source)
XLA Modules:
  0.0 103.1 jit_solution(7049134473919948288)
XLA Ops:
  6.6 0.9 copy-done
  7.4 5.6 %while.25 = (s32[]{:T(128)}, f32[64,1024]{1,0:T(8,128)S(1)}, s32[48,1024]{1,0:T(8,128)}, bf16[64,624]{1,0:T(8,128)(2,1)S(1)}, s32[]{:T(128)}, /*index=5*/s32[]{:T(128)}, s32[]{:T(128)}, s32[]{:T(128)}) while((s32[]{:T(128)}, f32[64,1024]{1,0:T(8,128)S(1)}, s32[48,1024]{1,0:T(8,128)}, bf16[64,624]{1,0:T(8,128)(2,1)S(1)}, s32[]{:T(128)}, ...), condition=%wide.region_1.0_spmd, body=%wide.region_0.0_spmd.sunk | while | flops 20926468 | bytes 2862547 | solution.py:61
  7.4 0.8 constant_dynamic-slice_fusion.6
  8.8 0.8 constant_dynamic-slice_fusion.6
  10.3 0.8 constant_dynamic-slice_fusion.6
  11.7 0.8 constant_dynamic-slice_fusion.6
  13.1 0.8 reshape.113
  14.0 24.0 %all-reduce.2.cloned.1.call-done = f32[16,4,1024]{2,1,0:T(4,128)} async-done(((f32[16,4,1024]{2,1,0:T(4,128)}), f32[16,4,1024]{2,1,0:T(4,128)}) %all-reduce.2.cloned.1.call-update) | async-done | bytes 262160 | tf_op jit(solution)/shard_map/psum | solution.py:120
  37.9 0.9 dynamic-slice_bitcast_fusion
  38.9 1.3 %collective-permute-start = (f32[4,1024]{1,0:T(4,128)S(1)}, f32[4,1024]{1,0:T(4,128)S(1)}, u32[]{:S(2)}, u32[]{:S(2)}) collective-permute-start(f32[4,1024]{1,0:T(4,128)S(1)} %get-tuple-element.245), channel_id=1, source_target_pairs={{0,1},{1,0},{2,3},{3,2},{4,5},{5,4},{6,7},{7,6},{8,9},{9,8},{10,11... | collective-permute-start | bytes 49160 | tf_op jit(solution)/shard_map/ppermute | solution.py:27
  40.4 1.4 %collective-permute-start.2 = (f32[4,1024]{1,0:T(4,128)S(1)}, f32[4,1024]{1,0:T(4,128)S(1)}, u32[]{:S(2)}, u32[]{:S(2)}) collective-permute-start(f32[4,1024]{1,0:T(4,128)S(1)} %get-tuple-element.243), channel_id=1, source_target_pairs={{0,3},{1,2},{2,1},{3,0},{4,7},{5,6},{6,5},{7,4},{8,11},{9,10},{10,... | collective-permute-start | bytes 49160 | tf_op jit(solution)/shard_map/ppermute | solution.py:27
  42.1 1.5 %collective-permute-start.4 = (f32[4,1024]{1,0:T(4,128)S(1)}, f32[4,1024]{1,0:T(4,128)S(1)}, u32[]{:S(2)}, u32[]{:S(2)}) collective-permute-start(f32[4,1024]{1,0:T(4,128)S(1)} %get-tuple-element.241), channel_id=1, source_target_pairs={{0,5},{1,4},{2,7},{3,6},{4,1},{5,0},{6,3},{7,2},{8,13},{9,12},{10,... | collective-permute-start | bytes 49160 | tf_op jit(solution)/shard_map/ppermute | solution.py:27
  43.9 2.4 %collective-permute-start.6 = (f32[4,1024]{1,0:T(4,128)S(1)}, f32[4,1024]{1,0:T(4,128)S(1)}, u32[]{:S(2)}, u32[]{:S(2)}) collective-permute-start(f32[4,1024]{1,0:T(4,128)S(1)} %get-tuple-element.239), channel_id=1, source_target_pairs={{0,7},{1,6},{2,5},{3,4},{4,3},{5,2},{6,1},{7,0},{8,15},{9,14},{10,... | collective-permute-start | bytes 49160 | tf_op jit(solution)/shard_map/ppermute | solution.py:27
  46.3 2.1 %collective-permute-start.7 = (f32[4,1024]{1,0:T(4,128)S(1)}, f32[4,1024]{1,0:T(4,128)S(1)}, u32[]{:S(2)}, u32[]{:S(2)}) collective-permute-start(f32[4,1024]{1,0:T(4,128)S(1)} %get-tuple-element.238), channel_id=1, source_target_pairs={{0,8},{1,9},{2,10},{3,11},{4,12},{5,13},{6,14},{7,15},{8,0},{9,1},... | collective-permute-start | bytes 49160 | tf_op jit(solution)/shard_map/ppermute | solution.py:27
  49.0 2.1 %collective-permute-start.9 = (f32[4,1024]{1,0:T(4,128)S(1)}, f32[4,1024]{1,0:T(4,128)S(1)}, u32[]{:S(2)}, u32[]{:S(2)}) collective-permute-start(f32[4,1024]{1,0:T(4,128)S(1)} %get-tuple-element.236), channel_id=1, source_target_pairs={{0,10},{1,11},{2,8},{3,9},{4,14},{5,15},{6,12},{7,13},{8,2},{9,3},... | collective-permute-start | bytes 49160 | tf_op jit(solution)/shard_map/ppermute | solution.py:27
  51.1 1.4 %collective-permute-start.10 = (f32[4,1024]{1,0:T(4,128)S(1)}, f32[4,1024]{1,0:T(4,128)S(1)}, u32[]{:S(2)}, u32[]{:S(2)}) collective-permute-start(f32[4,1024]{1,0:T(4,128)S(1)} %get-tuple-element.235), channel_id=1, source_target_pairs={{0,11},{1,10},{2,9},{3,8},{4,15},{5,14},{6,13},{7,12},{8,3},{9,2},... | collective-permute-start | bytes 49160 | tf_op jit(solution)/shard_map/ppermute | solution.py:27
  52.5 1.2 %collective-permute-start.11 = (f32[4,1024]{1,0:T(4,128)S(1)}, f32[4,1024]{1,0:T(4,128)S(1)}, u32[]{:S(2)}, u32[]{:S(2)}) collective-permute-start(f32[4,1024]{1,0:T(4,128)S(1)} %get-tuple-element.234), channel_id=1, source_target_pairs={{0,12},{1,13},{2,14},{3,15},{4,8},{5,9},{6,10},{7,11},{8,4},{9,5},... | collective-permute-start | bytes 49160 | tf_op jit(solution)/shard_map/ppermute | solution.py:27
  54.3 1.2 %collective-permute-start.13 = (f32[4,1024]{1,0:T(4,128)S(1)}, f32[4,1024]{1,0:T(4,128)S(1)}, u32[]{:S(2)}, u32[]{:S(2)}) collective-permute-start(f32[4,1024]{1,0:T(4,128)S(1)} %get-tuple-element.232), channel_id=1, source_target_pairs={{0,14},{1,15},{2,12},{3,13},{4,10},{5,11},{6,8},{7,9},{8,6},{9,7},... | collective-permute-start | bytes 49160 | tf_op jit(solution)/shard_map/ppermute | solution.py:27
  55.5 1.4 %collective-permute-start.14 = (f32[4,1024]{1,0:T(4,128)S(1)}, f32[4,1024]{1,0:T(4,128)S(1)}, u32[]{:S(2)}, u32[]{:S(2)}) collective-permute-start(f32[4,1024]{1,0:T(4,128)S(1)} %get-tuple-element.231), channel_id=1, source_target_pairs={{0,15},{1,14},{2,13},{3,12},{4,11},{5,10},{6,9},{7,8},{8,7},{9,6},... | collective-permute-start | bytes 49160 | tf_op jit(solution)/shard_map/ppermute | solution.py:27
  57.1 0.7 collective-permute-done.13
  57.8 2.0 %collective-permute-done.14 = f32[4,1024]{1,0:T(4,128)S(1)} collective-permute-done((f32[4,1024]{1,0:T(4,128)S(1)}, f32[4,1024]{1,0:T(4,128)S(1)}, u32[]{:S(2)}, u32[]{:S(2)}) %collective-permute-start.14) | collective-permute-done | bytes 16416 | tf_op jit(solution)/shard_map/ppermute | solution.py:27
  59.8 0.7 gather_fusion
  61.2 14.3 %all_to_all.16 = bf16[4,16,1024]{2,0,1:T(4,128)(2,1)S(1)} all-to-all(bf16[4,16,1024]{2,0,1:T(4,128)(2,1)S(1)} %fusion.11), channel_id=1, replica_groups=mesh['hap'=2,'snp'=16] {'snp'}, dimensions={1} | all-to-all | bytes 262144 | tf_op jit(solution)/shard_map/all_to_all | solution.py:123
  75.6 3.6 %collective-permute-start.15 = (bf16[64,256]{1,0:T(8,128)(2,1)S(1)}, bf16[64,256]{1,0:T(8,128)(2,1)S(1)}, u32[]{:S(2)}, u32[]{:S(2)}) collective-permute-start(bf16[64,256]{1,0:T(8,128)(2,1)S(1)} %get-tuple-element.248), channel_id=1, source_target_pairs={{0,1},{1,2},{2,3},{3,4},{4,5},{5,6},{6,7},{7,8},{8,9},{9,10},{10,1... | collective-permute-start | bytes 98312 | tf_op jit(solution)/shard_map/ppermute | solution.py:37
  79.2 1.9 %collective-permute-start.16 = (bf16[64,256]{1,0:T(8,128)(2,1)S(1)}, bf16[64,256]{1,0:T(8,128)(2,1)S(1)}, u32[]{:S(2)}, u32[]{:S(2)}) collective-permute-start(bf16[64,256]{1,0:T(8,128)(2,1)S(1)} %get-tuple-element.247), channel_id=1, source_target_pairs={{1,0},{2,1},{3,2},{4,3},{5,4},{6,5},{7,6},{8,7},{9,8},{10,9},{11,1... | collective-permute-start | bytes 98312 | tf_op jit(solution)/shard_map/ppermute | solution.py:40
  81.2 4.2 %collective-permute-done.16 = bf16[64,256]{1,0:T(8,128)(2,1)S(1)} collective-permute-done((bf16[64,256]{1,0:T(8,128)(2,1)S(1)}, bf16[64,256]{1,0:T(8,128)(2,1)S(1)}, u32[]{:S(2)}, u32[]{:S(2)}) %collective-permute-start.16) | collective-permute-done | bytes 32800 | tf_op jit(solution)/shard_map/ppermute | solution.py:40
  85.5 0.7 copy-done.1
  86.1 6.3 %while.26 = (s32[]{:T(128)}, f32[2,256]{1,0:T(2,128)S(1)}, s32[2]{0:T(128)S(1)}, s32[]{:T(128)}, s32[]{:T(128)}, /*index=5*/s32[2,1024]{1,0:T(2,128)S(1)}, s32[1...) while((s32[]{:T(128)}, f32[2,256]{1,0:T(2,128)S(1)}, ...), condition=%wide.region_9.10_spmd, body=%wide.region_6.9_spmd.sunk | while | flops 28510736 | bytes 194930 | solution.py:114
  86.1 0.6 dynamic_slice.160
  87.5 0.8 subtract_maximum_fusion.2
  90.6 0.8 subtract_maximum_fusion.2
  92.5 3.2 %all-gather = f32[2,1,512]{2,1,0:T(1,128)S(1)} all-gather(f32[1,1,512]{2,1,0:T(1,128)S(1)} %reshape.123), channel_id=1, replica_groups=mesh['hap'=2,'snp'=16] {'hap'}, dimensions={0}, use_global_device_ids=true | all-gather | bytes 6144 | tf_op jit(solution)/shard_map/all_gather | solution.py:139
  (98 shorter events, 8.7 us)
Async XLA Ops:
  6.5 31.4 %all-reduce.2.cloned.1.call-start = ((), (), s32[]{:S(2)}) async-start(), calls=%async_computation.1 | async-start | bytes 524288 | tf_op jit(solution)/shard_map/psum | solution.py:120
  6.5 0.9 copy-start
  38.9 4.8 %collective-permute-start = (f32[4,1024]{1,0:T(4,128)S(1)}, f32[4,1024]{1,0:T(4,128)S(1)}, u32[]{:S(2)}, u32[]{:S(2)}) collective-permute-start(f32[4,1024]{1,0:T(4,128)S(1)} %get-tuple-element.245), channel_id=1, source_target_pairs={{0,1},{1,0},{2,3},{3,2},{4,5},{5,4},{6,7},{7,6},{8,9},{9,8},{10,11... | collective-permute-start | bytes 49160 | tf_op jit(solution)/shard_map/ppermute | solution.py:27
  40.1 3.8 %collective-permute-start.1 = (f32[4,1024]{1,0:T(4,128)S(1)}, f32[4,1024]{1,0:T(4,128)S(1)}, u32[]{:S(2)}, u32[]{:S(2)}) collective-permute-start(f32[4,1024]{1,0:T(4,128)S(1)} %get-tuple-element.244), channel_id=1, source_target_pairs={{0,2},{1,3},{2,0},{3,1},{4,6},{5,7},{6,4},{7,5},{8,10},{9,11},{10,... | collective-permute-start | bytes 49160 | tf_op jit(solution)/shard_map/ppermute | solution.py:27
  40.4 5.9 %collective-permute-start.2 = (f32[4,1024]{1,0:T(4,128)S(1)}, f32[4,1024]{1,0:T(4,128)S(1)}, u32[]{:S(2)}, u32[]{:S(2)}) collective-permute-start(f32[4,1024]{1,0:T(4,128)S(1)} %get-tuple-element.243), channel_id=1, source_target_pairs={{0,3},{1,2},{2,1},{3,0},{4,7},{5,6},{6,5},{7,4},{8,11},{9,10},{10,... | collective-permute-start | bytes 49160 | tf_op jit(solution)/shard_map/ppermute | solution.py:27
  41.9 6.6 %collective-permute-start.3 = (f32[4,1024]{1,0:T(4,128)S(1)}, f32[4,1024]{1,0:T(4,128)S(1)}, u32[]{:S(2)}, u32[]{:S(2)}) collective-permute-start(f32[4,1024]{1,0:T(4,128)S(1)} %get-tuple-element.242), channel_id=1, source_target_pairs={{0,4},{1,5},{2,6},{3,7},{4,0},{5,1},{6,2},{7,3},{8,12},{9,13},{10,... | collective-permute-start | bytes 49160 | tf_op jit(solution)/shard_map/ppermute | solution.py:27
  42.1 6.9 %collective-permute-start.4 = (f32[4,1024]{1,0:T(4,128)S(1)}, f32[4,1024]{1,0:T(4,128)S(1)}, u32[]{:S(2)}, u32[]{:S(2)}) collective-permute-start(f32[4,1024]{1,0:T(4,128)S(1)} %get-tuple-element.241), channel_id=1, source_target_pairs={{0,5},{1,4},{2,7},{3,6},{4,1},{5,0},{6,3},{7,2},{8,13},{9,12},{10,... | collective-permute-start | bytes 49160 | tf_op jit(solution)/shard_map/ppermute | solution.py:27
  43.6 7.5 %collective-permute-start.5 = (f32[4,1024]{1,0:T(4,128)S(1)}, f32[4,1024]{1,0:T(4,128)S(1)}, u32[]{:S(2)}, u32[]{:S(2)}) collective-permute-start(f32[4,1024]{1,0:T(4,128)S(1)} %get-tuple-element.240), channel_id=1, source_target_pairs={{0,6},{1,7},{2,4},{3,5},{4,2},{5,3},{6,0},{7,1},{8,14},{9,15},{10,... | collective-permute-start | bytes 49160 | tf_op jit(solution)/shard_map/ppermute | solution.py:27
  43.9 8.6 %collective-permute-start.6 = (f32[4,1024]{1,0:T(4,128)S(1)}, f32[4,1024]{1,0:T(4,128)S(1)}, u32[]{:S(2)}, u32[]{:S(2)}) collective-permute-start(f32[4,1024]{1,0:T(4,128)S(1)} %get-tuple-element.239), channel_id=1, source_target_pairs={{0,7},{1,6},{2,5},{3,4},{4,3},{5,2},{6,1},{7,0},{8,15},{9,14},{10,... | collective-permute-start | bytes 49160 | tf_op jit(solution)/shard_map/ppermute | solution.py:27
  46.3 7.5 %collective-permute-start.7 = (f32[4,1024]{1,0:T(4,128)S(1)}, f32[4,1024]{1,0:T(4,128)S(1)}, u32[]{:S(2)}, u32[]{:S(2)}) collective-permute-start(f32[4,1024]{1,0:T(4,128)S(1)} %get-tuple-element.238), channel_id=1, source_target_pairs={{0,8},{1,9},{2,10},{3,11},{4,12},{5,13},{6,14},{7,15},{8,0},{9,1},... | collective-permute-start | bytes 49160 | tf_op jit(solution)/shard_map/ppermute | solution.py:27
  48.4 5.9 %collective-permute-start.8 = (f32[4,1024]{1,0:T(4,128)S(1)}, f32[4,1024]{1,0:T(4,128)S(1)}, u32[]{:S(2)}, u32[]{:S(2)}) collective-permute-start(f32[4,1024]{1,0:T(4,128)S(1)} %get-tuple-element.237), channel_id=1, source_target_pairs={{0,9},{1,8},{2,11},{3,10},{4,13},{5,12},{6,15},{7,14},{8,1},{9,0},... | collective-permute-start | bytes 49160 | tf_op jit(solution)/shard_map/ppermute | solution.py:27
  49.0 6.5 %collective-permute-start.9 = (f32[4,1024]{1,0:T(4,128)S(1)}, f32[4,1024]{1,0:T(4,128)S(1)}, u32[]{:S(2)}, u32[]{:S(2)}) collective-permute-start(f32[4,1024]{1,0:T(4,128)S(1)} %get-tuple-element.236), channel_id=1, source_target_pairs={{0,10},{1,11},{2,8},{3,9},{4,14},{5,15},{6,12},{7,13},{8,2},{9,3},... | collective-permute-start | bytes 49160 | tf_op jit(solution)/shard_map/ppermute | solution.py:27
  51.1 5.9 %collective-permute-start.10 = (f32[4,1024]{1,0:T(4,128)S(1)}, f32[4,1024]{1,0:T(4,128)S(1)}, u32[]{:S(2)}, u32[]{:S(2)}) collective-permute-start(f32[4,1024]{1,0:T(4,128)S(1)} %get-tuple-element.235), channel_id=1, source_target_pairs={{0,11},{1,10},{2,9},{3,8},{4,15},{5,14},{6,13},{7,12},{8,3},{9,2},... | collective-permute-start | bytes 49160 | tf_op jit(solution)/shard_map/ppermute | solution.py:27
  52.5 4.5 %collective-permute-start.11 = (f32[4,1024]{1,0:T(4,128)S(1)}, f32[4,1024]{1,0:T(4,128)S(1)}, u32[]{:S(2)}, u32[]{:S(2)}) collective-permute-start(f32[4,1024]{1,0:T(4,128)S(1)} %get-tuple-element.234), channel_id=1, source_target_pairs={{0,12},{1,13},{2,14},{3,15},{4,8},{5,9},{6,10},{7,11},{8,4},{9,5},... | collective-permute-start | bytes 49160 | tf_op jit(solution)/shard_map/ppermute | solution.py:27
  53.7 3.4 %collective-permute-start.12 = (f32[4,1024]{1,0:T(4,128)S(1)}, f32[4,1024]{1,0:T(4,128)S(1)}, u32[]{:S(2)}, u32[]{:S(2)}) collective-permute-start(f32[4,1024]{1,0:T(4,128)S(1)} %get-tuple-element.233), channel_id=1, source_target_pairs={{0,13},{1,12},{2,15},{3,14},{4,9},{5,8},{6,11},{7,10},{8,5},{9,4},... | collective-permute-start | bytes 49160 | tf_op jit(solution)/shard_map/ppermute | solution.py:27
  54.3 3.5 %collective-permute-start.13 = (f32[4,1024]{1,0:T(4,128)S(1)}, f32[4,1024]{1,0:T(4,128)S(1)}, u32[]{:S(2)}, u32[]{:S(2)}) collective-permute-start(f32[4,1024]{1,0:T(4,128)S(1)} %get-tuple-element.232), channel_id=1, source_target_pairs={{0,14},{1,15},{2,12},{3,13},{4,10},{5,11},{6,8},{7,9},{8,6},{9,7},... | collective-permute-start | bytes 49160 | tf_op jit(solution)/shard_map/ppermute | solution.py:27
  55.5 4.3 %collective-permute-start.14 = (f32[4,1024]{1,0:T(4,128)S(1)}, f32[4,1024]{1,0:T(4,128)S(1)}, u32[]{:S(2)}, u32[]{:S(2)}) collective-permute-start(f32[4,1024]{1,0:T(4,128)S(1)} %get-tuple-element.231), channel_id=1, source_target_pairs={{0,15},{1,14},{2,13},{3,12},{4,11},{5,10},{6,9},{7,8},{8,7},{9,6},... | collective-permute-start | bytes 49160 | tf_op jit(solution)/shard_map/ppermute | solution.py:27
  75.6 5.6 %collective-permute-start.15 = (bf16[64,256]{1,0:T(8,128)(2,1)S(1)}, bf16[64,256]{1,0:T(8,128)(2,1)S(1)}, u32[]{:S(2)}, u32[]{:S(2)}) collective-permute-start(bf16[64,256]{1,0:T(8,128)(2,1)S(1)} %get-tuple-element.248), channel_id=1, source_target_pairs={{0,1},{1,2},{2,3},{3,4},{4,5},{5,6},{6,7},{7,8},{8,9},{9,10},{10,1... | collective-permute-start | bytes 98312 | tf_op jit(solution)/shard_map/ppermute | solution.py:37
  79.2 6.1 %collective-permute-start.16 = (bf16[64,256]{1,0:T(8,128)(2,1)S(1)}, bf16[64,256]{1,0:T(8,128)(2,1)S(1)}, u32[]{:S(2)}, u32[]{:S(2)}) collective-permute-start(bf16[64,256]{1,0:T(8,128)(2,1)S(1)} %get-tuple-element.247), channel_id=1, source_target_pairs={{1,0},{2,1},{3,2},{4,3},{5,4},{6,5},{7,6},{8,7},{9,8},{10,9},{11,1... | collective-permute-start | bytes 98312 | tf_op jit(solution)/shard_map/ppermute | solution.py:40
  85.4 0.7 copy-start.1
Sparse Core Ops, SparseCore 0:
  14.0 23.8 all-reduce.1
